TPU v7x, 512 devices: a whole 4x8x8 slice. The times are simulated.
512 devices in a mesh: ab: 32 (over z, x), cd: 16 (over y, core).
Axes of the slice: x: 4, y: 8, z: 8, core: 2. Of those that a mesh axis runs over, the one named last changes fastest.
Arguments:
- amplitudes: float32 [512, 8192], P('ab', 'cd'), may hold values from -6 to 6
- integrals: float32 [65536, 8192], P('ab', 'cd'), may hold values from -0.125 to 0.125
- ij_pairs: int32 [512, 2], P('cd'), may hold values from 0 to 127
- ab_pairs: int32 [65536, 2], P('ab'), may hold values from 0 to 1535
- eps_occ: float32 [128], replicated, may hold values from -1.5 to -0.3
- eps_vir: float32 [1536], replicated, may hold values from 0.1 to 2.5
Outputs:
- ladder: float32 [512, 65536], P('cd', 'ab')
- update: float32 [512, 65536], P('cd', 'ab')
All inputs are finite; a program needn't handle non-finite values.
Results may differ from a plain program's by a relative error of at most 0.00015.
Values sent between devices are 32-bit elements; how exact they have to be, the bound alone decides.
A program may use at most 64 MiB of HBM per device.

v0:
```python
import jax
import jax.numpy as jnp
from jax import lax
from jax.sharding import PartitionSpec as P


def lookup_energy(indices, energies):
    positions = lax.broadcasted_iota(jnp.int32, (indices.shape[0], energies.shape[0]), 1)
    picked = jnp.where(indices[:, None] == positions, energies[None, :], jnp.float32(0.0))
    return jnp.sum(picked, axis=1)


def contract_rows(row_block, col_block):
    return lax.dot_general(
        row_block,
        col_block,
        (((1,), (1,)), ((), ())),
        precision=lax.Precision.HIGHEST,
        preferred_element_type=jnp.float32,
    )


def on_device(amplitudes, integrals, ij_pairs, ab_pairs, eps_occ, eps_vir):
    partial_value = contract_rows(lax.all_gather(amplitudes, "ab", axis=0, tiled=True), integrals)
    ladder = lax.psum_scatter(partial_value, "cd", scatter_dimension=0, tiled=True)
    first_occ = lookup_energy(ij_pairs[:, 0], eps_occ)[:, None]
    second_occ = lookup_energy(ij_pairs[:, 1], eps_occ)[:, None]
    first_vir = lookup_energy(ab_pairs[:, 0], eps_vir)[None, :]
    second_vir = lookup_energy(ab_pairs[:, 1], eps_vir)[None, :]
    denominator = first_occ + second_occ - first_vir - second_vir
    update = ladder / denominator
    return (ladder, update)


def solution(mesh):
    in_specs = (P("ab", "cd"), P("ab", "cd"), P("cd", None), P("ab", None), P(), P())
    out_specs = (P("cd", "ab"), P("cd", "ab"))
    return jax.shard_map(
        on_device, mesh=mesh, in_specs=in_specs, out_specs=out_specs, check_vma=False
    )
```

profile of v0, /device:TPU:27, one launch (start us, length us, event | category | flops | bytes accessed | tf_op | source)
XLA Modules:
  0.0 179.7 jit_solution(8097404686899207612)
XLA Ops:
  7.2 0.0 all-gather.2.cloned.1.call-start
  7.2 0.7 all-gather.2.cloned.1.call-update
  7.9 0.0 reduce-scatter.2.cloned.1.call-start
  7.9 84.6 %all-gather.2.cloned.1.call-done = f32[512,512]{1,0:T(8,128)} async-done(((f32[16,512]{1,0:T(8,128)}), f32[512,512]{1,0:T(8,128)}) %all-gather.2.cloned.1.call-update) | async-done | bytes 1048592 | tf_op jit(solution)/shard_map/all_gather | solution.py:24
  92.5 10.4 %fusion.1 = f32[512,2048]{1,0:T(8,128)} fusion(f32[512,512]{1,0:T(8,128)} %all-gather.2.cloned.1.call-done, f32[2048,512]{1,0:T(8,128)} %param.7), kind=kOutput, calls=%fused_computation.12 | convolution fusion | flops 6442450944 | bytes 9437184 | tf_op jit(solution)/shard_map/dot_general | solution.py:14
  102.9 0.0 copy-start.1
  102.9 0.0 copy-start.2
  102.9 0.0 copy-start
  102.9 0.0 copy-start.3
  102.9 0.0 reduce-scatter.2.cloned.1.call-update
  102.9 0.6 copy-done.1
  103.5 0.0 copy-done.2
  103.5 0.2 select_reduce_fusion.2
  103.7 0.0 copy-done
  103.8 0.0 copy-done.3
  103.8 3.9 %select_reduce_fusion.1 = (f32[2048]{0:T(1024)S(1)}, f32[2048]{0:T(1024)S(1)}) fusion(f32[1536]{0:T(1024)S(1)} %copy-done.3, s32[2048]{0:T(1024)S(1)} %bitcast.9, s32[2048]{0:T(1024)S(1)} %bitcast.8), kind=kLoop, calls=%fused_computation.2 | loop fusion | flops 18870272 | bytes 38912 | tf_op jit(solution)/shard_map/reduce_sum | solution.py:10
  107.7 63.4 %reduce-scatter.2.cloned.1.call-done = f32[32,2048]{1,0:T(8,128)} async-done(((f32[512,2048]{1,0:T(8,128)}), f32[32,2048]{1,0:T(8,128)}) %reduce-scatter.2.cloned.1.call-update) | async-done | bytes 262160 | tf_op jit(solution)/shard_map/reduce_scatter | solution.py:25
  171.1 1.8 subtract_divide_fusion
  (3 shorter events, 0.0 us)
Async XLA Ops:
  7.2 85.3 %all-gather.2.cloned.1.call-start = ((), (), s32[]{:S(2)}) async-start(), calls=%async_computation.1 | async-start | bytes 1081344 | tf_op jit(solution)/shard_map/all_gather | solution.py:24
  7.9 163.2 %reduce-scatter.2.cloned.1.call-start = ((), (), s32[]{:S(2)}) async-start(), calls=%async_computation.2 | async-start | bytes 4456448 | tf_op jit(solution)/shard_map/reduce_scatter | solution.py:25
  102.9 0.7 copy-start.1
  102.9 0.7 copy-start.2
  102.9 0.9 copy-start
  102.9 0.9 copy-start.3
Sparse Core Ops, SparseCore 0:
  11.2 81.2 all-gather.1
  103.0 67.9 reduce-scatter.1
where the time goes:
time: 180 us
  waiting for transfers between devices  149 us (83%)
  between operations  14.1 us (8%)
  matrix products  10.4 us (6%)
  other arithmetic  5.86 us (3%)
    all_gather x1, waiting for transfers between devices, on_device(): lax.all_gather(amplitudes, 'ab', axis=0, tiled=True)  84.6 us
    reduce_scatter x1, waiting for transfers between devices, on_device(): lax.psum_scatter(partial_value, 'cd', scatter_dimension=0, tiled=True)  63.4 us
    dot_general x1, matrix products, contract_rows(): lax.dot_general(row_block, col_block, (((1,), (1,)), ((), ())), precision...  10.4 us
    reduce_sum x2, other arithmetic, lookup_energy(): return jnp.sum(picked, axis=1)  4.09 us
  transfers between devices with their start and end apart: 2, of which 2 were waited for; matrix products, arithmetic and copies ran while one was open for 2% of the time, Pallas kernels for 0%

commit v1 on v0

--- a/solution.py
+++ b/solution.py
@@ -2,6 +2,13 @@
 import jax.numpy as jnp
 from jax import lax
 from jax.sharding import PartitionSpec as P
+
+
+def use_the_column(xs):
+    n_dev_all = lax.axis_size("ab")
+    by_rank = tuple((n_dev_all if at == 0 else 1 for at in range(xs.ndim)))
+    a_now = jnp.tile(xs, by_rank)
+    return lax.all_to_all(a_now, axis_name="ab", split_axis=0, concat_axis=0, tiled=True)
 
 
 def lookup_energy(indices, energies):
@@ -21,7 +28,7 @@
 
 
 def on_device(amplitudes, integrals, ij_pairs, ab_pairs, eps_occ, eps_vir):
-    partial_value = contract_rows(lax.all_gather(amplitudes, "ab", axis=0, tiled=True), integrals)
+    partial_value = contract_rows(use_the_column(amplitudes), integrals)
     ladder = lax.psum_scatter(partial_value, "cd", scatter_dimension=0, tiled=True)
     first_occ = lookup_energy(ij_pairs[:, 0], eps_occ)[:, None]
     second_occ = lookup_energy(ij_pairs[:, 1], eps_occ)[:, None]

time: 180 us -> 131 us (0.73)
  the two profiles are of different devices: /device:TPU:27 before, /device:TPU:29 now
where the time goes in v1:
time: 131 us; the launch traced here: 130 us
  waiting for transfers between devices  59 us (45%)
  blocking collectives  39.6 us (30%)
  between operations  14.1 us (11%)
  matrix products  10.1 us (8%)
  other arithmetic  5.86 us (4%)
  local copies, waits for them, and re-layouts  1.54 us (1%)
    reduce_scatter x1, waiting for transfers between devices, on_device(): lax.psum_scatter(partial_value, 'cd', scatter_dimension=0, tiled=True)  58.9 us
    all_to_all x1, blocking collectives, use_the_column(): lax.all_to_all(a_now, axis_name='ab', split_axis=0, concat_axis=0, tiled=...  39.6 us
    dot_general x1, matrix products, contract_rows(): lax.dot_general(row_block, col_block, (((1,), (1,)), ((), ())), precision...  10.1 us
    reduce_sum x2, other arithmetic, lookup_energy(): return jnp.sum(picked, axis=1)  4.09 us
  transfers between devices with their start and end apart: 1, of which 1 were waited for; matrix products, arithmetic and copies ran while one was open for 3% of the time, Pallas kernels for 0%

profile of v1, /device:TPU:29, one launch (start us, length us, event | category | flops | bytes accessed | tf_op | source)
XLA Modules:
  0.0 130.2 jit_solution(6418490993698102634)
XLA Ops:
  7.2 0.0 reduce-scatter.2.cloned.1.call-start
  7.2 0.9 tile.2
  8.1 39.6 %all_to_all.9 = f32[32,16,512]{2,1,0:T(8,128)S(1)} all-to-all(f32[32,16,512]{2,1,0:T(8,128)S(1)} %tile.2), channel_id=1, replica_groups=mesh['ab'=32,'cd'=16] {'ab'}, dimensions={0} | all-to-all | bytes 2097152 | tf_op jit(solution)/shard_map/all_to_all | solution.py:11
  47.7 10.1 %fusion.1 = f32[512,2048]{1,0:T(8,128)} fusion(f32[512,512]{1,0:T(8,128)S(1)} %bitcast.9, f32[2048,512]{1,0:T(8,128)} %param.7), kind=kOutput, calls=%fused_computation.12 | convolution fusion | flops 6442450944 | bytes 9437184 | tf_op jit(solution)/shard_map/dot_general | solution.py:21
  57.8 0.0 copy-start.1
  57.8 0.0 copy-start.2
  57.8 0.0 copy-start
  57.8 0.0 copy-start.3
  57.9 0.0 reduce-scatter.2.cloned.1.call-update
  57.9 0.6 copy-done.1
  58.5 0.0 copy-done.2
  58.5 0.2 select_reduce_fusion.2
  58.7 0.0 copy-done
  58.8 0.0 copy-done.3
  58.8 3.9 %select_reduce_fusion.1 = (f32[2048]{0:T(1024)S(1)}, f32[2048]{0:T(1024)S(1)}) fusion(f32[1536]{0:T(1024)S(1)} %copy-done.3, s32[2048]{0:T(1024)S(1)} %bitcast.11, s32[2048]{0:T(1024)S(1)} %bitcast.10), kind=kLoop, calls=%fused_computation.2 | loop fusion | flops 18870272 | bytes 38912 | tf_op jit(solution)/shard_map/reduce_sum | solution.py:17
  62.7 58.9 %reduce-scatter.2.cloned.1.call-done = f32[32,2048]{1,0:T(8,128)} async-done(((f32[512,2048]{1,0:T(8,128)}), f32[32,2048]{1,0:T(8,128)}) %reduce-scatter.2.cloned.1.call-update) | async-done | bytes 262160 | tf_op jit(solution)/shard_map/reduce_scatter | solution.py:32
  121.6 1.8 %subtract_divide_fusion = f32[32,2048]{1,0:T(8,128)} fusion(f32[32,2048]{1,0:T(8,128)} %reduce-scatter.2.cloned.1.call-done, f32[2048]{0:T(1024)S(1)} %get-tuple-element.3, f32[2048]{0:T(1024)S(1)} %get-tuple-element.2, f32[32]{0:T(128)S(1)} %add.10), kind=kLoop, calls=%fused_computation.4 | loop fusion | flops 196608 | bytes 540800 | tf_op jit(solution)/shard_map/div | solution.py:38
  (3 shorter events, 0.0 us)
Async XLA Ops:
  7.2 114.5 %reduce-scatter.2.cloned.1.call-start = ((), (), s32[]{:S(2)}) async-start(), calls=%async_computation.2 | async-start | bytes 4456448 | tf_op jit(solution)/shard_map/reduce_scatter | solution.py:32
  57.8 0.7 copy-start.1
  57.8 0.7 copy-start.2
  57.8 0.9 copy-start
  57.8 0.9 copy-start.3
Sparse Core Ops, SparseCore 0:
  58.0 63.5 reduce-scatter.1
